TPU v7x, 512 devices: a whole 4x8x8 slice. The times are simulated.
512 devices in a mesh: row: 16 (over y, core), col: 32 (over z, x).
Axes of the slice: x: 4, y: 8, z: 8, core: 2. Of those that a mesh axis runs over, the one named last changes fastest.
Arguments:
- matrix: float32 [4, 16, 256, 2, 32, 256], P(None, 'row', None, None, 'col'), as said below
- vectors: float32 [4, 16, 256, 256], P(None, 'row'), may hold values from -0.046875 to 0.046875
- t_factor: float32 [256, 256], replicated, as said below
Outputs:
- updated: float32 [4, 16, 256, 2, 32, 256], P(None, 'row', None, None, 'col')
Inputs may be any that keep to these rules, and one draw needn't show every extreme that they name: matrix is exactly symmetric as an 16384 x 16384 matrix: entry (i, j) equals entry (j, i). t_factor is upper triangular with its diagonal between 0.5 and 1.5.
All inputs are finite; a program needn't handle non-finite values.
Results may differ from a plain program's by a relative error of at most 0.000068.
Values sent between devices are 32-bit elements; how exact they have to be, the bound alone decides.
A program may use at most 64 MiB of HBM per device.

v0:
```python
import jax
import jax.numpy as jnp
from jax import lax
from jax.sharding import PartitionSpec as P


def spread(value, axis, root):
    mine = lax.axis_index(axis) == root
    return lax.psum(jnp.where(mine, value, jnp.zeros_like(value)), axis)


def product(left, right):
    return jnp.dot(left, right, precision=lax.Precision.HIGHEST, preferred_element_type=jnp.float32)


def per_device(matrix, vectors, t_factor):
    block_rows = vectors.shape[0]
    block_size = vectors.shape[2]
    block_cols = matrix.shape[3]
    row_devs = lax.axis_size("row")
    col_devs = lax.axis_size("col")
    col_ratio = col_devs // row_devs
    row_pos = lax.axis_index("row")
    col_pos = lax.axis_index("col")
    top_block = vectors[0, 0]
    unit_top = jnp.tril(top_block, -1) + jnp.eye(block_size, dtype=jnp.float32)
    first_block = jnp.where(row_pos == 0, unit_top, top_block)
    blocks = jnp.concatenate([first_block[None], vectors[1:, 0]], axis=0)
    chosen_ids = col_ratio * jnp.arange(block_cols, dtype=jnp.int32) + col_pos // row_devs
    source_row = col_pos % row_devs
    chosen = jnp.take(blocks, chosen_ids, axis=0)
    col_vecs = spread(chosen, "row", source_row).reshape(block_cols * block_size, block_size)
    row_vecs = blocks.reshape(block_rows * block_size, block_size)
    local_tile = matrix.reshape(block_rows * block_size, block_cols * block_size)
    summed = lax.psum(product(local_tile, col_vecs), "col")
    applied = product(summed, t_factor)
    inner = lax.psum(product(row_vecs.T, applied), "row")
    middle = product(t_factor.T, inner)
    coupled_rows = applied - 0.5 * product(row_vecs, middle)
    coupled_blocks = jnp.take(
        coupled_rows.reshape(block_rows, block_size, block_size), chosen_ids, axis=0
    )
    coupled_cols = spread(coupled_blocks, "row", source_row).reshape(
        block_cols * block_size, block_size
    )
    result = local_tile - product(row_vecs, coupled_cols.T) - product(coupled_rows, col_vecs.T)
    return result.reshape(matrix.shape)


def solution(mesh):
    in_specs = (P(None, "row", None, None, "col", None), P(None, "row", None, None), P())
    out_specs = P(None, "row", None, None, "col", None)
    return jax.shard_map(
        per_device, mesh=mesh, in_specs=in_specs, out_specs=out_specs, check_vma=False
    )
```

profile of v0, /device:TPU:1, one launch (start us, length us, event | category | flops | bytes accessed | tf_op | source)
XLA Modules:
  0.0 565.3 jit_solution(9547505962765150211)
XLA Ops:
  6.5 0.0 copy-start
  6.6 1.2 slice_bitcast_fusion
  7.8 1.1 bitcast_select_fusion
  8.9 0.0 copy-start.3
  8.9 0.1 pad_maximum_fusion
  9.0 1.4 gather_fusion
  10.4 1.9 select_select_fusion.1
  12.3 0.0 all-reduce.5.cloned.1.call-update
  12.3 0.0 all-reduce.7.cloned.1.call-start
  12.4 8.1 %reduce = f32[4,256,2,256]{3,2,1,0:T(2,128)} reduce(f32[4,1,256,2,1,256]{5,4,3,2,1,0:T(1,128)S(1)} %copy-done.3, f32[]{:T(128)} %constant.58), dimensions={1,4}, to_apply=%param.5.reduce_sub_computation | reduce | bytes 4194308 | tf_op args[0]
  20.5 1.8 copy.5
  22.2 111.7 %all-reduce.5.cloned.1.call-done = f32[512,256]{1,0:T(8,128)} async-done(((f32[512,256]{1,0:T(8,128)}), f32[512,256]{1,0:T(8,128)}) %all-reduce.5.cloned.1.call-update) | async-done | bytes 524304 | tf_op jit(solution)/shard_map/psum | solution.py:9
  133.9 5.5 convolution_bitcast_fusion
  139.4 0.0 all-reduce.7.cloned.1.call-update
  139.4 0.2 all-reduce.9.cloned.1.call-start
  139.7 158.1 %all-reduce.7.cloned.1.call-done = f32[1024,256]{0,1:T(8,128)} async-done(((f32[1024,256]{0,1:T(8,128)}), f32[1024,256]{0,1:T(8,128)}) %all-reduce.7.cloned.1.call-update) | async-done | bytes 1048592 | tf_op jit(solution)/shard_map/psum | solution.py:35
  297.7 3.0 fusion.2
  300.8 0.0 copy-start.1
  300.8 1.0 copy-done.1
  301.7 2.5 fusion.3
  304.3 0.0 all-reduce.9.cloned.1.call-update
  304.3 0.0 all-reduce.11.cloned.1.call-start
  304.3 116.9 %all-reduce.9.cloned.1.call-done = f32[256,256]{1,0:T(8,128)} async-done(((f32[256,256]{1,0:T(8,128)}), f32[256,256]{1,0:T(8,128)}) %all-reduce.9.cloned.1.call-update) | async-done | bytes 262160 | tf_op jit(solution)/shard_map/psum | solution.py:37
  421.3 1.5 fusion.4
  422.8 3.2 fusion
  426.0 2.6 gather_fusion.1
  428.6 1.9 select_select_fusion
  430.6 0.0 all-reduce.11.cloned.1.call-update
  430.6 117.0 %all-reduce.11.cloned.1.call-done = f32[512,256]{1,0:T(8,128)} async-done(((f32[512,256]{1,0:T(8,128)}), f32[512,256]{1,0:T(8,128)}) %all-reduce.11.cloned.1.call-update) | async-done | bytes 524304 | tf_op jit(solution)/shard_map/psum | solution.py:9
  547.6 3.0 fusion.5
  550.7 3.4 subtract_subtract_fusion
  554.1 4.7 reshape.111
  (11 shorter events, 0.0 us)
Async XLA Ops:
  6.5 291.2 %copy-start = (f32[256,256]{1,0:T(8,128)S(1)}, f32[256,256]{1,0:T(8,128)}, u32[]{:S(2)}) copy-start(f32[256,256]{1,0:T(8,128)} %param.7) | copy-start | bytes 786436
  6.5 127.4 %all-reduce.5.cloned.1.call-start = ((), (), s32[]{:S(2)}) async-start(), calls=%async_computation | async-start | bytes 1048576 | tf_op jit(solution)/shard_map/psum | solution.py:9
  8.9 3.5 copy-start.3
  12.3 285.4 %all-reduce.7.cloned.1.call-start = ((), (), s32[]{:S(2)}) async-start(), calls=%async_computation.1 | async-start | bytes 2097152 | tf_op jit(solution)/shard_map/psum | solution.py:35
  139.4 281.8 %all-reduce.9.cloned.1.call-start = ((), (), s32[]{:S(2)}) async-start(), calls=%async_computation.2 | async-start | bytes 524288 | tf_op jit(solution)/shard_map/psum | solution.py:37
  300.8 1.0 copy-start.1
  304.3 243.3 %all-reduce.11.cloned.1.call-start = ((), (), s32[]{:S(2)}) async-start(), calls=%async_computation.3 | async-start | bytes 1048576 | tf_op jit(solution)/shard_map/psum | solution.py:9
  547.6 3.0 copy-start.2
  547.6 3.0 copy-start.4
Sparse Core Ops, SparseCore 0:
  12.5 121.3 all-reduce.4
  139.6 158.1 all-reduce.6
  304.4 116.7 all-reduce.8
  430.7 116.8 all-reduce.10
where the time goes:
time: 566 us; the launch traced here: 565 us
  waiting for transfers between devices  504 us (89%)
  matrix products  22.3 us (4%)
  between operations  13.3 us (2%)
  other arithmetic  13.1 us (2%)
  local copies, waits for them, and re-layouts  12.6 us (2%)
    psum x2, waiting for transfers between devices, spread(): return lax.psum(jnp.where(mine, value, jnp.zeros_like(value)), axis)  229 us
    psum x1, waiting for transfers between devices, per_device(): summed = lax.psum(product(local_tile, col_vecs), 'col')  158 us
    psum x1, waiting for transfers between devices, per_device(): inner = lax.psum(product(row_vecs.T, applied), 'row')  117 us
    dot_general x7, matrix products, product(): jnp.dot(left, right, precision=lax.Precision.HIGHEST, preferred_element_t...  22.3 us
  transfers between devices with their start and end apart: 4, of which 4 were waited for; matrix products, arithmetic and copies ran while one was open for 2% of the time, Pallas kernels for 0%

commit v1 on v0

--- a/solution.py
+++ b/solution.py
@@ -2,6 +2,12 @@
 import jax.numpy as jnp
 from jax import lax
 from jax.sharding import PartitionSpec as P
+
+
+def summed_here(shard, mesh_axis):
+    shards = lax.all_gather(shard, mesh_axis, axis=0, tiled=False)
+    total = shards.sum(axis=0)
+    return total
 
 
 def spread(value, axis, root):
@@ -34,7 +40,7 @@
     local_tile = matrix.reshape(block_rows * block_size, block_cols * block_size)
     summed = lax.psum(product(local_tile, col_vecs), "col")
     applied = product(summed, t_factor)
-    inner = lax.psum(product(row_vecs.T, applied), "row")
+    inner = summed_here(product(row_vecs.T, applied), "row")
     middle = product(t_factor.T, inner)
     coupled_rows = applied - 0.5 * product(row_vecs, middle)
     coupled_blocks = jnp.take(

time: 566 us -> 496 us (0.88)
  waiting for transfers between devices: 504 us -> 430 us
    psum x1 -> x0, waiting for transfers between devices: 117 us -> none  [per_device(): inner = lax.psum(product(row_vecs.T, applied), 'row')]
    all_gather x0 -> x1, waiting for transfers between devices: none -> 46.5 us  [summed_here(): shards = lax.all_gather(shard, mesh_axis, axis=0, tiled=False)]
where the time goes in v1:
time: 496 us; the launch traced here: 495 us
  waiting for transfers between devices  430 us (87%)
  matrix products  22.2 us (4%)
  other arithmetic  16.3 us (3%)
  between operations  13.3 us (3%)
  local copies, waits for them, and re-layouts  12.6 us (3%)
    psum x2, waiting for transfers between devices, spread(): return lax.psum(jnp.where(mine, value, jnp.zeros_like(value)), axis)  226 us
    psum x1, waiting for transfers between devices, per_device(): summed = lax.psum(product(local_tile, col_vecs), 'col')  158 us
    all_gather x1, waiting for transfers between devices, summed_here(): shards = lax.all_gather(shard, mesh_axis, axis=0, tiled=False)  46.5 us
    dot_general x7, matrix products, product(): jnp.dot(left, right, precision=lax.Precision.HIGHEST, preferred_element_t...  22.2 us
  transfers between devices with their start and end apart: 4, of which 4 were waited for; matrix products, arithmetic and copies ran while one was open for 2% of the time, Pallas kernels for 0%

profile of v1, /device:TPU:1, one launch (start us, length us, event | category | flops | bytes accessed | tf_op | source)
XLA Modules:
  0.0 495.2 jit_solution(4810285379709199058)
XLA Ops:
  6.6 1.2 slice_bitcast_fusion
  7.8 1.1 bitcast_select_fusion
  8.9 0.0 copy-start.3
  8.9 0.1 pad_maximum_fusion
  9.0 1.4 gather_fusion
  10.4 1.9 select_select_fusion.1
  12.3 0.0 all-reduce.4.cloned.1.call-update
  12.3 0.0 all-reduce.6.cloned.1.call-start
  12.4 8.1 %reduce = f32[4,256,2,256]{3,2,1,0:T(2,128)} reduce(f32[4,1,256,2,1,256]{5,4,3,2,1,0:T(1,128)S(1)} %copy-done.3, f32[]{:T(128)} %constant.59), dimensions={1,4}, to_apply=%param.5.reduce_sub_computation | reduce | bytes 4194308 | tf_op args[0]
  20.5 1.8 copy.5
  22.2 111.7 %all-reduce.4.cloned.1.call-done = f32[512,256]{1,0:T(8,128)} async-done(((f32[512,256]{1,0:T(8,128)}), f32[512,256]{1,0:T(8,128)}) %all-reduce.4.cloned.1.call-update) | async-done | bytes 524304 | tf_op jit(solution)/shard_map/psum | solution.py:15
  133.9 5.5 %convolution_bitcast_fusion = f32[1024,256]{0,1:T(8,128)} fusion(f32[512,256]{1,0:T(8,128)} %all-reduce.4.cloned.1.call-done, f32[1024,512]{1,0:T(8,128)S(1)} %bitcast.36), kind=kOutput, calls=%fused_computation.3 | convolution fusion | flops 1610612736 | bytes 3670016 | tf_op jit(solution)/shard_map/dot_general | solution.py:19
  139.4 0.0 all-reduce.6.cloned.1.call-update
  139.4 0.2 all-gather.3.cloned.1.call-start
  139.7 158.1 %all-reduce.6.cloned.1.call-done = f32[1024,256]{0,1:T(8,128)} async-done(((f32[1024,256]{0,1:T(8,128)}), f32[1024,256]{0,1:T(8,128)}) %all-reduce.6.cloned.1.call-update) | async-done | bytes 1048592 | tf_op jit(solution)/shard_map/psum | solution.py:41
  297.7 3.0 fusion.2
  300.8 0.0 copy-start.1
  300.8 1.0 copy-done.1
  301.7 2.5 fusion.3
  304.2 0.0 all-gather.3.cloned.1.call-update
  304.3 0.0 all-reduce.8.cloned.1.call-start
  304.3 46.5 %all-gather.3.cloned.1.call-done = f32[4096,256]{1,0:T(8,128)} async-done(((f32[256,256]{1,0:T(8,128)}), f32[4096,256]{1,0:T(8,128)}) %all-gather.3.cloned.1.call-update) | async-done | bytes 4194320 | tf_op jit(solution)/shard_map/all_gather | solution.py:8
  350.8 3.2 reduce_sum.9
  354.0 1.5 fusion.4
  355.5 3.2 fusion
  358.8 2.6 gather_fusion.1
  361.4 1.9 select_select_fusion
  363.3 0.0 all-reduce.8.cloned.1.call-update
  363.3 114.2 %all-reduce.8.cloned.1.call-done = f32[512,256]{1,0:T(8,128)} async-done(((f32[512,256]{1,0:T(8,128)}), f32[512,256]{1,0:T(8,128)}) %all-reduce.8.cloned.1.call-update) | async-done | bytes 524304 | tf_op jit(solution)/shard_map/psum | solution.py:15
  477.5 3.0 fusion.5
  480.6 3.4 subtract_subtract_fusion
  484.0 4.7 reshape.112
  (12 shorter events, 0.0 us)
Async XLA Ops:
  6.5 291.2 %copy-start = (f32[256,256]{1,0:T(8,128)S(1)}, f32[256,256]{1,0:T(8,128)}, u32[]{:S(2)}) copy-start(f32[256,256]{1,0:T(8,128)} %param.7) | copy-start | bytes 786436
  6.5 127.4 %all-reduce.4.cloned.1.call-start = ((), (), s32[]{:S(2)}) async-start(), calls=%async_computation | async-start | bytes 1048576 | tf_op jit(solution)/shard_map/psum | solution.py:15
  8.9 3.5 copy-start.3
  12.3 285.4 %all-reduce.6.cloned.1.call-start = ((), (), s32[]{:S(2)}) async-start(), calls=%async_computation.1 | async-start | bytes 2097152 | tf_op jit(solution)/shard_map/psum | solution.py:41
  139.4 211.4 %all-gather.3.cloned.1.call-start = ((), (), s32[]{:S(2)}) async-start(), calls=%async_computation.3 | async-start | bytes 4456448 | tf_op jit(solution)/shard_map/all_gather | solution.py:8
  300.8 1.0 copy-start.1
  304.3 173.3 %all-reduce.8.cloned.1.call-start = ((), (), s32[]{:S(2)}) async-start(), calls=%async_computation.2 | async-start | bytes 1048576 | tf_op jit(solution)/shard_map/psum | solution.py:15
  477.5 3.0 copy-start.2
  477.5 3.0 copy-start.4
Sparse Core Ops, SparseCore 0:
  12.5 121.3 all-reduce.3
  139.6 158.1 all-reduce.5
  304.4 46.3 all-gather.2
  363.4 114.0 all-reduce.7
